TPU v7x, 128 devices: a whole 4x4x4 slice. The times are simulated.
128 devices in a mesh: seq: 16 (over x_hi, y, core), fsdp: 2 (over x_lo), dp: 4 (over z).
Axes of the slice: x: 4 (x_hi: 2, x_lo: 2; x = x_hi * 2 + x_lo), y: 4, z: 4, core: 2. Of those that a mesh axis runs over, the one named last changes fastest.
Arguments:
- queries: bfloat16 [8, 4096, 4096], P(('fsdp', 'dp'), 'seq'), may hold values from -160 to 160
- hidden: bfloat16 [8, 4096, 8192], P(('fsdp', 'dp'), 'seq'), may hold values from -8 to 8
- key_weight: bfloat16 [8192, 512], P('fsdp'), may hold values from -1 to 1
- doc_lengths: int32 [8, 32], P(('fsdp', 'dp')), may hold values from 1 to 256, 4096 in all within a row
- entropy_cot: bfloat16 [8, 4096, 32], P(('fsdp', 'dp'), 'seq'), may hold values from -600 to 600
Outputs:
- entropy: float32 [8, 4096, 32], P(('fsdp', 'dp'), 'seq')
- grad_queries: bfloat16 [8, 4096, 4096], P(('fsdp', 'dp'), 'seq')
- grad_key_weight: bfloat16 [8192, 512], P('fsdp')
Inputs may be any that keep to these rules, and one draw needn't show every extreme that they name: `doc_lengths`: each sequence's 32 documents are packed in order, their lengths sum to 4096, and the longest is exactly 256.
All inputs are finite; a program needn't handle non-finite values.
Results may differ from a plain program's by a relative error of at most 0.0088.
Values may be sent and summed in bfloat16 or wider, within the bound.
No kernel may reach another device: no remote copies, remote signals or barrier semaphores. Data moves between devices by JAX's collectives and lax.ppermute only.
A program may use at most 128 MiB of HBM per device.

v0:
```python
import jax
import jax.numpy as jnp
from jax import lax
from jax.sharding import PartitionSpec as P

QH = 32
KVH = 4
HD = 128


def document_index(lengths, seq_len):
    ends = jnp.cumsum(lengths)
    position = jnp.arange(seq_len, dtype=jnp.int32)
    return jnp.sum((ends[None, :] <= position[:, None]).astype(jnp.int32), axis=1)


def attend(queries, key_rows, cotangent, doc_index, doc_len):
    row_count, key_heads, group_size, head_size = queries.shape
    full_len = key_rows.shape[0]
    block_rows = min(512, row_count)
    window = block_rows + doc_len
    factor = head_size ** (-0.5)
    keys_padded = jnp.concatenate(
        [jnp.zeros((doc_len, key_heads, head_size), key_rows.dtype), key_rows], axis=0
    )
    index_padded = jnp.concatenate([jnp.full((doc_len,), -1, jnp.int32), doc_index], axis=0)

    def one_block(step_index, state_now):
        entropy, grad_query, grad_key = state_now
        row_start = (step_index * block_rows).astype(jnp.int32)
        query_block = lax.dynamic_slice_in_dim(queries, row_start, block_rows, 0)
        weight_block = lax.dynamic_slice_in_dim(cotangent, row_start, block_rows, 0).astype(
            jnp.float32
        )
        key_block = lax.dynamic_slice_in_dim(keys_padded, row_start, window, 0)
        key_docs = lax.dynamic_slice_in_dim(index_padded, row_start, window, 0)
        query_docs = lax.dynamic_slice_in_dim(doc_index, row_start, block_rows, 0)
        query_pos = row_start + jnp.arange(block_rows, dtype=jnp.int32)
        key_pos = row_start - doc_len + jnp.arange(window, dtype=jnp.int32)
        visible = (query_docs[:, None] == key_docs[None, :]) & (
            key_pos[None, :] <= query_pos[:, None]
        )
        scores = (
            jnp.einsum("rkgd,wkd->kgrw", query_block, key_block, preferred_element_type=jnp.float32)
            * factor
        )
        scores = jnp.where(visible, scores, -1e30)
        row_max = jnp.max(scores, axis=-1, keepdims=True)
        powers = jnp.exp(scores - row_max)
        denominator = jnp.sum(powers, axis=-1, keepdims=True)
        probability = powers / denominator
        mean_score = jnp.sum(jnp.where(visible, probability * scores, 0.0), axis=-1, keepdims=True)
        block_entropy = (row_max + jnp.log(denominator) - mean_score)[..., 0]
        row_weight = jnp.transpose(weight_block, (1, 2, 0))[..., None]
        slope = jnp.where(visible, row_weight * probability * (mean_score - scores), 0.0).astype(
            jnp.bfloat16
        )
        query_part = (
            jnp.einsum("kgrw,wkd->rkgd", slope, key_block, preferred_element_type=jnp.float32)
            * factor
        )
        key_part = (
            jnp.einsum("kgrw,rkgd->wkd", slope, query_block, preferred_element_type=jnp.float32)
            * factor
        )
        entropy = lax.dynamic_update_slice_in_dim(
            entropy, jnp.transpose(block_entropy, (2, 0, 1)), row_start, 0
        )
        grad_query = lax.dynamic_update_slice_in_dim(grad_query, query_part, row_start, 0)
        previous = lax.dynamic_slice_in_dim(grad_key, row_start, window, 0)
        grad_key = lax.dynamic_update_slice_in_dim(grad_key, previous + key_part, row_start, 0)
        return (entropy, grad_query, grad_key)

    initial = (
        jnp.zeros((row_count, key_heads, group_size), jnp.float32),
        jnp.zeros((row_count, key_heads, group_size, head_size), jnp.float32),
        jnp.zeros((full_len + doc_len, key_heads, head_size), jnp.float32),
    )
    entropy, grad_query, grad_key = lax.fori_loop(0, row_count // block_rows, one_block, initial)
    return (entropy, grad_query, grad_key[doc_len:])


def shards(queries, hidden, key_weight, doc_lengths, entropy_cot):
    tokens = hidden[0]
    local_rows = tokens.shape[0]
    seq_parts = lax.axis_size("seq")
    seq_len = local_rows * seq_parts
    group_size = QH // KVH
    doc_index = document_index(doc_lengths[0], seq_len)
    columns = tokens
    key_local = jnp.dot(
        columns,
        lax.all_gather(key_weight, "fsdp", axis=0, tiled=True),
        preferred_element_type=jnp.float32,
    ).astype(jnp.bfloat16)
    query_local = queries[0]
    cot_local = entropy_cot[0]
    share = QH // seq_parts
    outgoing = jnp.broadcast_to(
        key_local.reshape(local_rows, KVH, 1, HD), (local_rows, KVH, group_size, HD)
    )
    outgoing = outgoing.reshape(local_rows, KVH * group_size * HD)
    query_heads, key_heads_seq, cot_heads = (
        lax.all_to_all(query_local, "seq", split_axis=1, concat_axis=0, tiled=True),
        lax.all_to_all(outgoing, "seq", split_axis=1, concat_axis=0, tiled=True),
        lax.all_to_all(cot_local, "seq", split_axis=1, concat_axis=0, tiled=True),
    )
    key_count = key_heads_seq.shape[1] // HD
    entropy, grad_query, grad_key = attend(
        query_heads.reshape(seq_len, key_count, share // key_count, HD),
        key_heads_seq.reshape(seq_len, key_count, HD),
        cot_heads.reshape(seq_len, key_count, share // key_count),
        doc_index,
        local_rows,
    )
    grad_local, key_grad_local, entropy_local = (
        lax.all_to_all(
            grad_query.reshape(seq_len, share * HD), "seq", split_axis=0, concat_axis=1, tiled=True
        ),
        lax.all_to_all(
            grad_key.reshape(seq_len, key_count * HD),
            "seq",
            split_axis=0,
            concat_axis=1,
            tiled=True,
        ),
        lax.all_to_all(
            entropy.reshape(seq_len, share), "seq", split_axis=0, concat_axis=1, tiled=True
        ),
    )
    key_grad = jnp.sum(key_grad_local.reshape(local_rows, KVH, -1, HD), axis=2).reshape(
        local_rows, KVH * HD
    )
    key_grad_low = key_grad.astype(jnp.bfloat16)
    columns = tokens
    term_rows = lax.psum_scatter(
        lax.dot_general(
            columns, key_grad_low, (((0,), (0,)), ((), ())), preferred_element_type=jnp.float32
        ),
        "fsdp",
        scatter_dimension=0,
        tiled=True,
    )
    summed = lax.psum(term_rows, ("seq", "dp"))
    norm_factor = (seq_len * lax.axis_size("fsdp") * lax.axis_size("dp")) ** (-0.5)
    weight_grad = (summed * norm_factor).astype(jnp.bfloat16)
    return (
        entropy_local.reshape(1, local_rows, QH),
        grad_local.astype(jnp.bfloat16).reshape(1, local_rows, QH * HD),
        weight_grad,
    )


def solution(mesh):
    return jax.shard_map(
        shards,
        mesh=mesh,
        in_specs=(
            P(("fsdp", "dp"), "seq", None),
            P(("fsdp", "dp"), "seq", None),
            P("fsdp", None),
            P(("fsdp", "dp"), None),
            P(("fsdp", "dp"), "seq", None),
        ),
        out_specs=(P(("fsdp", "dp"), "seq", None), P(("fsdp", "dp"), "seq", None), P("fsdp", None)),
        check_vma=False,
    )
```

profile of v0, /device:TPU:0, one launch (start us, length us, event | category | flops | bytes accessed | tf_op | source)
XLA Modules:
  0.0 1256.6 jit_solution(18081824443787886025)
XLA Ops:
  11.2 7.1 all-to-all-start.1
  18.3 114.7 %all-gather.2.cloned.1.call-done = bf16[8192,512]{1,0:T(8,128)(2,1)} async-done(((bf16[4096,512]{1,0:T(8,128)(2,1)}), bf16[8192,512]{1,0:T(8,128)(2,1)}) %all-gather.2.cloned.1.call-update) | async-done | bytes 8388624 | tf_op jit(solution)/shard_map/all_gather | solution.py:93
  133.0 7.0 fusion.41
  141.7 8.3 all-to-all-start
  150.9 28.5 %all-to-all-done = bf16[256,16,256]{0,2,1:T(8,128)(2,1)} async-done(((bf16[256,16,256]{0,2,1:T(8,128)(2,1)}), bf16[256,16,256]{0,2,1:T(8,128)(2,1)}, u32[]{:S(2)}, u32[]{:S(2)}) %all-to-all-start) | async-done | bytes 2097184 | tf_op jit(solution)/shard_map/all_to_all | solution.py:105
  179.3 6.3 all-to-all-start.2
  188.5 4.2 reshape.222
  192.7 4.1 copy.82
  204.4 88.0 %while.19 = (s32[]{:T(128)}, f32[4096,2,1]{0,1,2:T(2,128)}, bf16[4096,2,1,128]{0,3,1,2:T(8,128)(2,1)S(1)}, f32[4352,2,128]{0,2,1:T(8,128)}, s32[4096]{0:T(1024)S...) while((s32[]{:T(128)}, f32[4096,2,1]{0,1,2:T(2,128)}, ...), condition=%wide.region_6.7_spmd, body=%wide.region_2.6_spmd.sunk | while | flops 630850816 | bytes 21601552 | solution.py:79
  244.7 3.7 fusion.61
  255.7 3.7 fusion.61
  277.7 3.7 fusion.61
  288.7 3.7 fusion.61
  299.1 58.8 %all_to_all.93 = f32[16,256,256]{1,2,0:T(8,128)} all-to-all(f32[16,256,256]{1,2,0:T(8,128)S(1)} %copy.90), channel_id=1, replica_groups=mesh['seq'=16,'fsdp'=2,'dp'=4] {'seq'}, dimensions={0} | all-to-all | bytes 8388608 | tf_op jit(solution)/shard_map/all_to_all | solution.py:120
  360.4 10.3 convolution_bitcast_fusion
  370.7 189.8 %reduce-scatter.2.cloned.1.call-done = f32[4096,512]{0,1:T(8,128)} async-done(((f32[8192,512]{0,1:T(8,128)}), f32[4096,512]{0,1:T(8,128)}) %reduce-scatter.2.cloned.1.call-update) | async-done | bytes 8388624 | tf_op jit(solution)/shard_map/reduce_scatter | solution.py:136
  560.6 6.5 all-to-all-start.3
  569.1 4.3 copy.98
  574.7 5.9 all-to-all-start.4
  581.2 29.5 %all-to-all-done.4 = bf16[16,256,256]{2,1,0:T(8,128)(2,1)S(1)} async-done(((bf16[16,256,256]{2,1,0:T(8,128)(2,1)}), bf16[16,256,256]{2,1,0:T(8,128)(2,1)S(1)}, u32[]{:S(2)}, u32[]{:S(2)}) %all-to-all-start.4) | async-done | bytes 2097184 | tf_op jit(solution)/shard_map/all_to_all | solution.py:117
  613.0 4.1 copy.91
  617.1 620.1 %all-reduce.4.cloned.1.call-done = f32[4096,512]{0,1:T(8,128)} async-done(((f32[4096,512]{0,1:T(8,128)}), f32[4096,512]{0,1:T(8,128)}) %all-reduce.4.cloned.1.call-update) | async-done | bytes 8388624 | tf_op jit(solution)/shard_map/psum | solution.py:144
  1237.3 6.4 multiply_convert_fusion
  1243.6 6.4 copy.92
  (129 shorter events, 105.7 us)
Async XLA Ops:
  7.2 1.6 copy-start
  7.2 125.8 %all-gather.2.cloned.1.call-start = ((), (), s32[]{:S(2)}) async-start(), calls=%async_computation.7 | async-start | bytes 12582912 | tf_op jit(solution)/shard_map/all_gather | solution.py:93
  11.2 128.9 %all-to-all-start.1 = ((bf16[256,16,256]{0,2,1:T(8,128)(2,1)}), bf16[256,16,256]{0,2,1:T(8,128)(2,1)S(1)}, u32[]{:S(2)}, u32[]{:S(2)}) async-start(bf16[256,16,256]{0,2,1:T(8,128)(2,1)} %bitcast.144), calls=%async_computation.1 | async-start | bytes 4194304 | tf_op jit(solution)/shard_map/all_to_all | solution.py:104
  140.1 9.9 copy-start.2
  140.1 10.1 copy-start.1
  141.7 37.6 %all-to-all-start = ((bf16[256,16,256]{0,2,1:T(8,128)(2,1)}), bf16[256,16,256]{0,2,1:T(8,128)(2,1)}, u32[]{:S(2)}, u32[]{:S(2)}) async-start(bf16[256,16,256]{0,2,1:T(8,128)(2,1)} %bitcast.145), calls=%async_computation | async-start | bytes 4194304 | tf_op jit(solution)/shard_map/all_to_all | solution.py:105
  179.3 21.9 %all-to-all-start.2 = ((bf16[256,16,2]{0,2,1:T(2,128)(2,1)}), bf16[256,16,2]{0,2,1:T(2,128)(2,1)S(1)}, u32[]{:S(2)}, u32[]{:S(2)}) async-start(bf16[256,16,2]{0,2,1:T(2,128)(2,1)} %all_to_all.76), calls=%async_computation.2 | async-start | bytes 32768 | tf_op jit(solution)/shard_map/all_to_all | solution.py:106
  185.6 374.9 %reduce-scatter.2.cloned.1.call-start = ((), (), s32[]{:S(2)}) async-start(), calls=%async_computation.8 | async-start | bytes 25165824 | tf_op jit(solution)/shard_map/reduce_scatter | solution.py:136
  370.7 866.6 %all-reduce.4.cloned.1.call-start = ((), (), s32[]{:S(2)}) async-start(), calls=%async_computation.9 | async-start | bytes 16777216 | tf_op jit(solution)/shard_map/psum | solution.py:144
  560.6 14.1 %all-to-all-start.3 = ((f32[16,256,2]{1,2,0:T(2,128)}), f32[16,256,2]{1,2,0:T(2,128)S(1)}, u32[]{:S(2)}, u32[]{:S(2)}) async-start(f32[16,256,2]{1,2,0:T(2,128)} %bitcast.20), calls=%async_computation.3 | async-start | bytes 65536 | tf_op jit(solution)/shard_map/all_to_all | solution.py:127
  574.7 36.0 %all-to-all-start.4 = ((bf16[16,256,256]{2,1,0:T(8,128)(2,1)}), bf16[16,256,256]{2,1,0:T(8,128)(2,1)S(1)}, u32[]{:S(2)}, u32[]{:S(2)}) async-start(bf16[16,256,256]{2,1,0:T(8,128)(2,1)} %copy.98), calls=%async_computation.4 | async-start | bytes 4194304 | tf_op jit(solution)/shard_map/all_to_all | solution.py:117
Sparse Core Ops, SparseCore 0:
  9.7 123.2 all-gather.1
  370.8 189.6 reduce-scatter.1
  563.2 674.0 all-reduce.3
where the time goes:
time: 1260 us
  waiting for transfers between devices  985 us (78%)
  matrix products  81.7 us (6%)
  blocking collectives  58.8 us (5%)
  local copies, waits for them, and re-layouts  51.6 us (4%)
  starting transfers between devices  34.4 us (3%)
  other arithmetic  31.4 us (2%)
  between operations  13.9 us (1%)
    psum x1, waiting for transfers between devices, shards(): summed = lax.psum(term_rows, ('seq', 'dp'))  620 us
    reduce_scatter x1, waiting for transfers between devices, shards(): lax.psum_scatter(lax.dot_general(columns, key_grad_low, (((0,), (0,)), ((...  190 us
    all_gather x1, waiting for transfers between devices, shards(): lax.all_gather(key_weight, 'fsdp', axis=0, tiled=True)  115 us
    all_to_all x1, blocking collectives, shards(): lax.all_to_all(grad_key.reshape(seq_len, key_count * HD), 'seq', split_ax...  58.8 us
    all_to_all x1, waiting for transfers between devices, shards(): lax.all_to_all(grad_query.reshape(seq_len, share * HD), 'seq', split_axis...  29.5 us
    dot_general x8, matrix products, one_block(): jnp.einsum('kgrw,rkgd->wkd', slope, query_block, preferred_element_type=j...  29.3 us
    all_to_all x1, waiting for transfers between devices, shards(): lax.all_to_all(outgoing, 'seq', split_axis=1, concat_axis=0, tiled=True)  28.5 us
  transfers between devices with their start and end apart: 8, of which 6 were waited for; matrix products, arithmetic and copies ran while one was open for 3% of the time, Pallas kernels for 0%

commit v1 on v0

--- a/solution.py
+++ b/solution.py
@@ -141,7 +141,7 @@
         scatter_dimension=0,
         tiled=True,
     )
-    summed = lax.psum(term_rows, ("seq", "dp"))
+    summed = lax.psum(lax.psum(term_rows, "dp"), "seq")
     norm_factor = (seq_len * lax.axis_size("fsdp") * lax.axis_size("dp")) ** (-0.5)
     weight_grad = (summed * norm_factor).astype(jnp.bfloat16)
     return (

time: 1260 us -> 930 us (0.74)
  waiting for transfers between devices: 985 us -> 656 us
    psum x1 -> x2, waiting for transfers between devices: 620 us -> 280 us  [shards(): summed = lax.psum(lax.psum(term_rows, 'dp'), 'seq')]
  transfers between devices with their start and end apart: 8 -> 9, of which waited for: 6 -> 7; matrix products, arithmetic and copies ran while one was open for 3% -> 4% of each run, Pallas kernels for 0% -> 0%
where the time goes in v1:
time: 930 us; the launch traced here: 928 us
  waiting for transfers between devices  656 us (71%)
  matrix products  81.7 us (9%)
  blocking collectives  58.8 us (6%)
  local copies, waits for them, and re-layouts  51.6 us (6%)
  starting transfers between devices  34.6 us (4%)
  other arithmetic  31.3 us (3%)
  between operations  13.9 us (1%)
    psum x2, waiting for transfers between devices, shards(): summed = lax.psum(lax.psum(term_rows, 'dp'), 'seq')  280 us
    reduce_scatter x1, waiting for transfers between devices, shards(): lax.psum_scatter(lax.dot_general(columns, key_grad_low, (((0,), (0,)), ((...  190 us
    all_gather x1, waiting for transfers between devices, shards(): lax.all_gather(key_weight, 'fsdp', axis=0, tiled=True)  115 us
    all_to_all x1, blocking collectives, shards(): lax.all_to_all(grad_key.reshape(seq_len, key_count * HD), 'seq', split_ax...  58.8 us
    all_to_all x1, waiting for transfers between devices, shards(): lax.all_to_all(grad_query.reshape(seq_len, share * HD), 'seq', split_axis...  41.5 us
    dot_general x8, matrix products, one_block(): jnp.einsum('kgrw,rkgd->wkd', slope, query_block, preferred_element_type=j...  29.3 us
    all_to_all x1, waiting for transfers between devices, shards(): lax.all_to_all(outgoing, 'seq', split_axis=1, concat_axis=0, tiled=True)  28.5 us
    dot_general x8, matrix products, one_block(): jnp.einsum('kgrw,wkd->rkgd', slope, key_block, preferred_element_type=jnp...  19.7 us
  transfers between devices with their start and end apart: 9, of which 7 were waited for; matrix products, arithmetic and copies ran while one was open for 4% of the time, Pallas kernels for 0%

profile of v1, /device:TPU:0, one launch (start us, length us, event | category | flops | bytes accessed | tf_op | source)
XLA Modules:
  0.0 928.4 jit_solution(15943684415915102141)
XLA Ops:
  11.2 7.1 all-to-all-start.1
  18.3 114.7 %all-gather.2.cloned.1.call-done = bf16[8192,512]{1,0:T(8,128)(2,1)} async-done(((bf16[4096,512]{1,0:T(8,128)(2,1)}), bf16[8192,512]{1,0:T(8,128)(2,1)}) %all-gather.2.cloned.1.call-update) | async-done | bytes 8388624 | tf_op jit(solution)/shard_map/all_gather | solution.py:93
  133.0 7.0 fusion.41
  141.7 8.3 all-to-all-start
  150.9 28.5 %all-to-all-done = bf16[256,16,256]{0,2,1:T(8,128)(2,1)} async-done(((bf16[256,16,256]{0,2,1:T(8,128)(2,1)}), bf16[256,16,256]{0,2,1:T(8,128)(2,1)}, u32[]{:S(2)}, u32[]{:S(2)}) %all-to-all-start) | async-done | bytes 2097184 | tf_op jit(solution)/shard_map/all_to_all | solution.py:105
  179.3 6.3 all-to-all-start.2
  188.5 4.2 reshape.222
  192.7 4.1 copy.82
  204.4 88.0 %while.19 = (s32[]{:T(128)}, f32[4096,2,1]{0,1,2:T(2,128)}, bf16[4096,2,1,128]{0,3,1,2:T(8,128)(2,1)S(1)}, f32[4352,2,128]{0,2,1:T(8,128)}, s32[4096]{0:T(1024)S...) while((s32[]{:T(128)}, f32[4096,2,1]{0,1,2:T(2,128)}, ...), condition=%wide.region_6.7_spmd, body=%wide.region_2.6_spmd.sunk | while | flops 630850816 | bytes 21601552 | solution.py:79
  255.7 3.7 fusion.61
  277.7 3.7 fusion.61
  288.7 3.7 fusion.61
  299.1 58.8 %all_to_all.93 = f32[16,256,256]{1,2,0:T(8,128)} all-to-all(f32[16,256,256]{1,2,0:T(8,128)S(1)} %copy.90), channel_id=1, replica_groups=mesh['seq'=16,'fsdp'=2,'dp'=4] {'seq'}, dimensions={0} | all-to-all | bytes 8388608 | tf_op jit(solution)/shard_map/all_to_all | solution.py:120
  360.4 10.3 %convolution_bitcast_fusion = f32[8192,512]{0,1:T(8,128)} fusion(bf16[256,512]{0,1:T(8,128)(2,1)S(1)} %bitcast.150, bf16[1,256,8192]{2,1,0:T(8,128)(2,1)} %param.8), kind=kOutput, calls=%fused_computation.33 | convolution fusion | flops 2147483648 | bytes 21233664 | tf_op jit(solution)/shard_map/dot_general | solution.py:137
  370.7 189.8 %reduce-scatter.2.cloned.1.call-done = f32[4096,512]{0,1:T(8,128)} async-done(((f32[8192,512]{0,1:T(8,128)}), f32[4096,512]{0,1:T(8,128)}) %reduce-scatter.2.cloned.1.call-update) | async-done | bytes 8388624 | tf_op jit(solution)/shard_map/reduce_scatter | solution.py:136
  560.6 164.0 %all-reduce.5.cloned.1.call-done = f32[4096,512]{0,1:T(8,128)} async-done(((f32[4096,512]{0,1:T(8,128)}), f32[4096,512]{0,1:T(8,128)}) %all-reduce.5.cloned.1.call-update) | async-done | bytes 8388624 | tf_op jit(solution)/shard_map/psum | solution.py:144
  724.7 6.8 all-to-all-start.3
  733.5 4.3 copy.98
  739.2 5.8 all-to-all-start.4
  745.6 41.5 %all-to-all-done.4 = bf16[16,256,256]{2,1,0:T(8,128)(2,1)S(1)} async-done(((bf16[16,256,256]{2,1,0:T(8,128)(2,1)}), bf16[16,256,256]{2,1,0:T(8,128)(2,1)S(1)}, u32[]{:S(2)}, u32[]{:S(2)}) %all-to-all-start.4) | async-done | bytes 2097184 | tf_op jit(solution)/shard_map/all_to_all | solution.py:117
  789.5 4.1 copy.91
  793.6 115.6 %all-reduce.7.cloned.1.call-done = f32[4096,512]{0,1:T(8,128)} async-done(((f32[4096,512]{0,1:T(8,128)}), f32[4096,512]{0,1:T(8,128)}) %all-reduce.7.cloned.1.call-update) | async-done | bytes 8388624 | tf_op jit(solution)/shard_map/psum | solution.py:144
  909.2 6.3 multiply_convert_fusion
  915.5 6.4 copy.92
  (132 shorter events, 109.5 us)
Async XLA Ops:
  7.2 1.6 copy-start
  7.2 125.8 %all-gather.2.cloned.1.call-start = ((), (), s32[]{:S(2)}) async-start(), calls=%async_computation.7 | async-start | bytes 12582912 | tf_op jit(solution)/shard_map/all_gather | solution.py:93
  11.2 128.9 %all-to-all-start.1 = ((bf16[256,16,256]{0,2,1:T(8,128)(2,1)}), bf16[256,16,256]{0,2,1:T(8,128)(2,1)S(1)}, u32[]{:S(2)}, u32[]{:S(2)}) async-start(bf16[256,16,256]{0,2,1:T(8,128)(2,1)} %bitcast.144), calls=%async_computation.1 | async-start | bytes 4194304 | tf_op jit(solution)/shard_map/all_to_all | solution.py:104
  140.1 9.9 %copy-start.2 = (s32[1,32]{1,0:T(1,128)S(1)}, s32[1,32]{1,0:T(1,128)}, u32[]{:S(2)}) copy-start(s32[1,32]{1,0:T(1,128)} %param.10) | copy-start | bytes 388
  140.1 10.1 %copy-start.1 = (bf16[1,256,32]{1,2,0:T(8,128)(2,1)S(1)}, bf16[1,256,32]{1,2,0:T(8,128)(2,1)}, u32[]{:S(2)}) copy-start(bf16[1,256,32]{1,2,0:T(8,128)(2,1)} %param.11) | copy-start | bytes 49156
  141.7 37.6 %all-to-all-start = ((bf16[256,16,256]{0,2,1:T(8,128)(2,1)}), bf16[256,16,256]{0,2,1:T(8,128)(2,1)}, u32[]{:S(2)}, u32[]{:S(2)}) async-start(bf16[256,16,256]{0,2,1:T(8,128)(2,1)} %bitcast.145), calls=%async_computation | async-start | bytes 4194304 | tf_op jit(solution)/shard_map/all_to_all | solution.py:105
  179.3 21.9 %all-to-all-start.2 = ((bf16[256,16,2]{0,2,1:T(2,128)(2,1)}), bf16[256,16,2]{0,2,1:T(2,128)(2,1)S(1)}, u32[]{:S(2)}, u32[]{:S(2)}) async-start(bf16[256,16,2]{0,2,1:T(2,128)(2,1)} %all_to_all.76), calls=%async_computation.2 | async-start | bytes 32768 | tf_op jit(solution)/shard_map/all_to_all | solution.py:106
  185.6 374.9 %reduce-scatter.2.cloned.1.call-start = ((), (), s32[]{:S(2)}) async-start(), calls=%async_computation.8 | async-start | bytes 25165824 | tf_op jit(solution)/shard_map/reduce_scatter | solution.py:136
  370.7 354.0 %all-reduce.5.cloned.1.call-start = ((), (), s32[]{:S(2)}) async-start(), calls=%async_computation.9 | async-start | bytes 16777216 | tf_op jit(solution)/shard_map/psum | solution.py:144
  560.6 348.6 %all-reduce.7.cloned.1.call-start = ((), (), s32[]{:S(2)}) async-start(), calls=%async_computation.10 | async-start | bytes 16777216 | tf_op jit(solution)/shard_map/psum | solution.py:144
  724.7 14.5 %all-to-all-start.3 = ((f32[16,256,2]{1,2,0:T(2,128)}), f32[16,256,2]{1,2,0:T(2,128)S(1)}, u32[]{:S(2)}, u32[]{:S(2)}) async-start(f32[16,256,2]{1,2,0:T(2,128)} %bitcast.20), calls=%async_computation.3 | async-start | bytes 65536 | tf_op jit(solution)/shard_map/all_to_all | solution.py:127
  739.2 47.9 %all-to-all-start.4 = ((bf16[16,256,256]{2,1,0:T(8,128)(2,1)}), bf16[16,256,256]{2,1,0:T(8,128)(2,1)S(1)}, u32[]{:S(2)}, u32[]{:S(2)}) async-start(bf16[16,256,256]{2,1,0:T(8,128)(2,1)} %copy.98), calls=%async_computation.4 | async-start | bytes 4194304 | tf_op jit(solution)/shard_map/all_to_all | solution.py:117
Sparse Core Ops, SparseCore 0:
  9.7 123.2 all-gather.1
  370.8 189.6 reduce-scatter.1
  563.2 161.4 all-reduce.4
  727.2 181.9 all-reduce.6
